TPU v7x, 32 devices: a whole 2x2x4 slice. The times are simulated.
32 devices in a mesh: frames: 4 (over y, core), win: 8 (over z, x).
Axes of the slice: x: 2, y: 2, z: 4, core: 2. Of those that a mesh axis runs over, the one named last changes fastest.
Arguments:
- memberships: float32 [8, 256, 4096], P('win', 'frames'), as said below
- lag_times: int32 [8], P('win'), may hold values from 1 to 8, as said below
- segment_ids: int32 [8, 256], P('win'), may hold values from 0 to 7, never falling along the last dimension, each value on 1 to 128 neighbouring positions
- bias_codes: int32 [8, 4096], P('win'), may hold values from 0 to 511
Outputs:
- free_energy: float32 [4096], P('frames')
- log_multipliers: float32 [8, 4096], P('win', 'frames')
Inputs may be any that keep to these rules, and one draw needn't show every extreme that they name: Positive; each frame's memberships sum to one up to rounding. `lag_times`: some window's lag time is 8.
All inputs are finite; a program needn't handle non-finite values.
Results may differ from a plain program's by a relative error of at most 0.00041.
Values may be sent and summed in bfloat16 or wider, within the bound.
No kernel may reach another device: no remote copies, remote signals or barrier semaphores. Data moves between devices by JAX's collectives and lax.ppermute only.
A program may use at most 64 MiB of HBM per device.

v0:
```python
import jax
import jax.numpy as jnp
from jax import lax
from jax.sharding import PartitionSpec as P

LAGMAX = 8
ITERS = 2
bias_unit = 1.0 / 128.0


def shifted(block, axis, distance):
    devices = range(lax.axis_size(axis))
    route = [(i - distance, i) for i in devices if i - distance in devices]
    return lax.ppermute(block, axis, route)


def split_rows(block, frames_dev, lag_time, valid_all):
    width = frames_dev + LAGMAX
    number = block.shape[0] // width
    states = block.shape[1]
    shaped = block.reshape(number, width, states)
    current = shaped[:, :frames_dev].reshape(number * frames_dev, states)
    later = lax.dynamic_slice_in_dim(shaped, lag_time, frames_dev, 1).reshape(
        number * frames_dev, states
    )
    later = jnp.where(valid_all[:, None], later, jnp.zeros((), later.dtype))
    return (current, later)


def add_pair(accumulated, current, later, first, rows):
    current_cols = lax.dynamic_slice_in_dim(current, first, rows, 1)
    later_cols = lax.dynamic_slice_in_dim(later, first, rows, 1)
    accumulated = jnp.einsum("tr,ts->rs", current_cols, later, preferred_element_type=jnp.float32)
    return accumulated + jnp.einsum(
        "tr,ts->rs", later_cols, current, preferred_element_type=jnp.float32
    )


def shards(memberships, lag_times, segment_ids, bias_codes):
    member = memberships[0].astype(jnp.bfloat16)
    lag_time = lag_times[0]
    segment_row = segment_ids[0]
    frames_dev = member.shape[0]
    states = member.shape[1]
    frames_all = segment_row.shape[0]
    rows = states // lax.axis_size("frames")
    position = lax.axis_index("frames")
    first = position * rows
    heading = shifted(member[:LAGMAX], "frames", -1)
    extended = jnp.concatenate([member, heading], axis=0)
    segment_ext = jnp.concatenate([segment_row, jnp.full((LAGMAX,), -1, jnp.int32)])
    valid_all = segment_row == lax.dynamic_slice_in_dim(segment_ext, lag_time, frames_all, 0)
    empty = jnp.zeros((rows, states), jnp.float32)
    current, later = split_rows(
        lax.all_gather(extended, "frames", axis=0, tiled=True), frames_dev, lag_time, valid_all
    )
    sym_counts = add_pair(empty, current, later, first, rows)
    gammas = jnp.exp(-bias_codes[0].astype(jnp.float32) * bias_unit)
    gamma_rows = lax.dynamic_slice_in_dim(gammas, first, rows, 0)
    mult_rows = jnp.sum(sym_counts, axis=1) * 0.5
    mult_full = lax.all_gather(mult_rows, "frames", axis=0, tiled=True)
    window_total = jnp.sum(mult_full)
    count_rows = lax.psum(mult_rows, "win")
    weights = jnp.full((states,), 1.0 / states, jnp.float32)
    for sweep in range(ITERS):
        scaled = gammas * weights
        scaled_rows = lax.dynamic_slice_in_dim(scaled, first, rows, 0)
        denom = mult_rows[:, None] * scaled[None, :] + scaled_rows[:, None] * mult_full[None, :]
        ratios = sym_counts / denom
        new_rows = mult_rows * jnp.sum(ratios * scaled[None, :], axis=1)
        terms = gamma_rows * jnp.sum(ratios * mult_full[None, :], axis=1)
        term_rows = lax.psum(terms, "win")
        raw_rows = count_rows / term_rows
        if sweep + 1 < ITERS:
            raw_full, mult_full = (
                lax.all_gather(raw_rows, "frames", axis=0, tiled=True),
                lax.all_gather(new_rows, "frames", axis=0, tiled=True),
            )
        else:
            raw_full = lax.all_gather(raw_rows, "frames", axis=0, tiled=True)
        weights = raw_full / jnp.sum(raw_full)
        mult_rows = new_rows
    weight_rows = lax.dynamic_slice_in_dim(weights, first, rows, 0)
    free_energy = -jnp.log(states * weight_rows)
    log_multipliers = jnp.log(mult_rows * states / window_total)[None, :]
    return (free_energy, log_multipliers)


def solution(mesh):
    placed = (P("win", "frames", None), P("win"), P("win", None), P("win", None))
    return jax.shard_map(
        shards,
        mesh=mesh,
        in_specs=placed,
        out_specs=(P("frames"), P("win", "frames")),
        check_vma=False,
    )
```

profile of v0, /device:TPU:0, one launch (start us, length us, event | category | flops | bytes accessed | tf_op | source)
XLA Modules:
  0.0 147.7 jit_solution(16507466639481832255)
XLA Ops:
  7.2 0.0 all-gather.2.cloned.1.call-start
  7.2 1.3 convert_element_type.11
  8.5 1.3 collective-permute-start
  9.8 1.3 convert_bitcast_fusion
  11.1 0.6 collective-permute-done
  11.7 0.9 pad_maximum_fusion
  12.5 0.0 all-gather.2.cloned.1.call-update
  13.2 0.8 broadcast_multiply_fusion
  14.0 0.8 fusion.6
  14.8 25.7 %all-gather.2.cloned.1.call-done = bf16[288,4096]{1,0:T(8,128)(2,1)} async-done(((bf16[72,4096]{1,0:T(8,128)(2,1)}), bf16[288,4096]{1,0:T(8,128)(2,1)}) %all-gather.2.cloned.1.call-update) | async-done | bytes 2359312 | tf_op jit(solution)/shard_map/all_gather | solution.py:55
  40.5 2.9 %fusion.10 = (bf16[4,64,4096]{2,1,0:T(8,128)(2,1)S(1)}, bf16[4,64,4096]{2,1,0:T(8,128)(2,1)S(1)}) fusion(bf16[4,72,4096]{2,1,0:T(8,128)(2,1)} %bitcast.23, s32[]{:T(128)S(6)} %select_n.20), kind=kLoop, calls=%fused_computation.30 | loop fusion | bytes 8388612 | tf_op jit(solution)/shard_map/slice | solution.py:22
  43.4 0.0 copy-start.1
  43.4 0.4 bitcast_select_fusion
  43.8 0.9 copy-done.1
  44.8 8.1 %fusion.1 = f32[1024,4096]{1,0:T(8,128)} fusion(bf16[256,4096]{1,0:T(8,128)(2,1)S(1)} %bitcast_select_fusion, bf16[256,4096]{1,0:T(8,128)(2,1)S(1)} %bitcast.21, s32[]{:T(128)S(6)} %select_n.18), kind=kOutput, calls=%fused_computation.10 | convolution fusion | flops 2147483648 | bytes 19398660 | tf_op jit(solution)/shard_map/tr,ts->rs/dot_general | solution.py:33
  52.9 7.8 %fusion.11 = (f32[1024]{0:T(1024)S(1)}, f32[1024,4096]{1,0:T(8,128)S(1)}) fusion(f32[1024,4096]{1,0:T(8,128)} %fusion.1, bf16[256,4096]{1,0:T(8,128)(2,1)} %bitcast.22, bf16[256,4096]{1,0:T(8,128)(2,1)S(1)} %bitcast_select_fusion, s32[]{:T(128)S(6)} %select_n.18), kind=kOutput, calls=%fused_computation.31 | convolution fusion | flops 2155871232 | bytes 36179972 | tf_op jit(solution)/shard_map/tr,ts->rs/dot_general | solution.py:34
  60.7 0.0 copy-start
  60.7 5.2 %all_gather.16 = f32[4096]{0:T(1024)S(1)} all-gather(f32[1024]{0:T(1024)S(1)} %broadcast_multiply_fusion.1), channel_id=1, replica_groups=mesh['frames'=4,'win'=8] {'frames'}, dimensions={0}, use_global_device_ids=true | all-gather | bytes 20480 | tf_op jit(solution)/shard_map/all_gather | solution.py:61
  65.9 0.5 copy-done
  66.4 6.2 %multiply_reduce_fusion.2 = (f32[1024]{0:T(1024)S(1)}, f32[1024]{0:T(1024)S(1)}) fusion(f32[4096]{0:T(1024)S(1)} %all_gather.16, f32[4096]{0:T(1024)S(1)} %bitcast.26, f32[1024,4096]{1,0:T(8,128)S(1)} %get-tuple-element.13, f32[1024]{0:T(1024)S(1)} %dynamic-slice_multiply_fusion, f32[1024]{0:T(1024)S(1)} %broadcast_multiply_fusion.1), kind=kLoop, calls=%fused_computation.3 | loop fusion | flops 33552384 | bytes 16826368 | tf_op jit(solution)/shard_map/reduce_sum | solution.py:71
  72.6 5.2 %all_gather.18 = f32[4096]{0:T(1024)S(1)} all-gather(f32[1024]{0:T(1024)S(1)} %fusion.9), channel_id=1, replica_groups=mesh['frames'=4,'win'=8] {'frames'}, dimensions={0}, use_global_device_ids=true | all-gather | bytes 20480 | tf_op jit(solution)/shard_map/all_gather | solution.py:77
  77.8 21.6 %all-reduce.1 = (f32[1024]{0:T(1024)S(1)}, f32[1024]{0:T(1024)S(1)}) all-reduce(f32[1024]{0:T(1024)S(1)} %broadcast_multiply_fusion.1, f32[1024]{0:T(1024)S(1)} %mul.185), channel_id=1, replica_groups=mesh['frames'=4,'win'=8] {'win'}, use_global_device_ids=true, to_apply=%region_1.2 | all-reduce | flops 2048 | bytes 16384 | tf_op jit(solution)/shard_map/psum | solution.py:63
  99.4 5.2 %all_gather.17 = f32[4096]{0:T(1024)S(1)} all-gather(f32[1024]{0:T(1024)S(1)} %div.38), channel_id=1, replica_groups=mesh['frames'=4,'win'=8] {'frames'}, dimensions={0}, use_global_device_ids=true | all-gather | bytes 20480 | tf_op jit(solution)/shard_map/all_gather | solution.py:76
  104.6 0.6 reduce_sum.79
  105.2 0.6 reduce_sum.75
  105.8 0.7 divide_multiply_fusion
  106.5 9.0 %multiply_reduce_fusion = (f32[1024]{0:T(1024)S(1)}, f32[1024]{0:T(1024)S(1)}) fusion(f32[4096]{0:T(1024)S(1)} %divide_multiply_fusion, f32[4096]{0:T(1024)S(1)} %all_gather.18, f32[1024,4096]{1,0:T(8,128)} %copy-done, f32[1024]{0:T(1024)S(1)} %dynamic_slice.33, f32[1024]{0:T(1024)S(1)} %fusion.9), kind=kLoop, calls=%fused_computation | loop fusion | flops 33552384 | bytes 16826368 | tf_op jit(solution)/shard_map/reduce_sum | solution.py:70
  115.5 17.1 %psum.23 = f32[1024]{0:T(1024)S(1)} all-reduce(f32[1024]{0:T(1024)S(1)} %mul.193), channel_id=1, replica_groups=mesh['frames'=4,'win'=8] {'win'}, use_global_device_ids=true, to_apply=%region_7.8 | all-reduce | flops 1024 | bytes 8192 | tf_op jit(solution)/shard_map/psum | solution.py:72
  132.7 5.2 %all_gather.19 = f32[4096]{0:T(1024)S(1)} all-gather(f32[1024]{0:T(1024)S(1)} %div.42), channel_id=1, replica_groups=mesh['frames'=4,'win'=8] {'frames'}, dimensions={0}, use_global_device_ids=true | all-gather | bytes 20480 | tf_op jit(solution)/shard_map/all_gather | solution.py:80
  137.9 0.6 reduce_sum.77
  138.5 1.3 fusion.5
  139.7 1.2 divide_log_fusion
  (10 shorter events, 0.1 us)
Async XLA Ops:
  7.2 33.3 %all-gather.2.cloned.1.call-start = ((), (), s32[]{:S(2)}) async-start(), calls=%async_computation | async-start | bytes 2949120 | tf_op jit(solution)/shard_map/all_gather | solution.py:55
  8.5 3.1 %collective-permute-start = (bf16[8,4096]{1,0:T(8,128)(2,1)S(1)}, bf16[8,4096]{1,0:T(8,128)(2,1)S(1)}, u32[]{:S(2)}, u32[]{:S(2)}) collective-permute-start(bf16[8,4096]{1,0:T(8,128)(2,1)S(1)} %slice_bitcast_fusion), channel_id=1, source_target_pairs={{8,0},{16,8},{24,16},{9,1},{17,9},{25,17},{10,2},{18,10},{26,18},{... | collective-permute-start | bytes 196616 | tf_op jit(solution)/shard_map/ppermute | solution.py:14
  43.4 1.4 copy-start.1
  60.7 5.7 %copy-start = (f32[1024,4096]{1,0:T(8,128)}, f32[1024,4096]{1,0:T(8,128)S(1)}, u32[]{:S(2)}) copy-start(f32[1024,4096]{1,0:T(8,128)S(1)} %get-tuple-element.13) | copy-start | bytes 50331652
Sparse Core Ops, SparseCore 0:
  12.7 27.7 all-gather.1
where the time goes:
time: 148 us
  blocking collectives  59.6 us (40%)
  waiting for transfers between devices  26.2 us (18%)
  other arithmetic  25.5 us (17%)
  matrix products  15.9 us (11%)
  between operations  14.8 us (10%)
  local copies, waits for them, and re-layouts  4.38 us (3%)
    all_gather x1, waiting for transfers between devices, shards(): lax.all_gather(extended, 'frames', axis=0, tiled=True)  25.7 us
    psum x1, blocking collectives, shards(): count_rows = lax.psum(mult_rows, 'win')  21.6 us
    psum x1, blocking collectives, shards(): term_rows = lax.psum(terms, 'win')  17.1 us
    reduce_sum x1, other arithmetic, shards(): new_rows = mult_rows * jnp.sum(ratios * scaled[None, :], axis=1)  8.98 us
    dot_general x1, matrix products, add_pair(): jnp.einsum('tr,ts->rs', current_cols, later, preferred_element_type=jnp.f...  8.12 us
    dot_general x1, matrix products, add_pair(): jnp.einsum('tr,ts->rs', later_cols, current, preferred_element_type=jnp.f...  7.76 us
    reduce_sum x1, other arithmetic, shards(): terms = gamma_rows * jnp.sum(ratios * mult_full[None, :], axis=1)  6.19 us
    all_gather x1, blocking collectives, shards(): mult_full = lax.all_gather(mult_rows, 'frames', axis=0, tiled=True)  5.21 us
  transfers between devices with their start and end apart: 2, of which 2 were waited for; matrix products, arithmetic and copies ran while one was open for 2% of the time, Pallas kernels for 0%

commit v1 on v0

--- a/solution.py
+++ b/solution.py
@@ -1,11 +1,20 @@
+import functools
 import jax
 import jax.numpy as jnp
 from jax import lax
 from jax.sharding import PartitionSpec as P
+from jax.lax import all_gather
 
 LAGMAX = 8
 ITERS = 2
 bias_unit = 1.0 / 128.0
+
+
+def mix_works(own_rows, net_axis):
+    return all_gather(own_rows, net_axis).sum(axis=0)
+
+
+produce_column = functools.partial(mix_works, net_axis="win")
 
 
 def shifted(block, axis, distance):
@@ -69,7 +78,7 @@
         ratios = sym_counts / denom
         new_rows = mult_rows * jnp.sum(ratios * scaled[None, :], axis=1)
         terms = gamma_rows * jnp.sum(ratios * mult_full[None, :], axis=1)
-        term_rows = lax.psum(terms, "win")
+        term_rows = produce_column(terms)
         raw_rows = count_rows / term_rows
         if sweep + 1 < ITERS:
             raw_full, mult_full = (

time: 148 us -> 190 us (1.28)
  blocking collectives: 59.6 us -> 103 us
  matrix products: 15.9 us -> 11.2 us
  other arithmetic: 25.5 us -> 28.5 us
    all_gather x0 -> x2, blocking collectives: none -> 61.2 us  [mix_works(): return all_gather(own_rows, net_axis).sum(axis=0)]
    psum x1 -> x0, blocking collectives: 17.1 us -> none  [shards(): term_rows = lax.psum(terms, 'win')]
    dot_general x1, matrix products: 8.12 us -> 2.41 us  [add_pair(): jnp.einsum('tr,ts->rs', current_cols, later, preferred_element_type=jnp.f...]
    reduce_sum x1, other arithmetic: 6.19 us -> 9.14 us  [shards(): terms = gamma_rows * jnp.sum(ratios * mult_full[None, :], axis=1)]
where the time goes in v1:
time: 190 us; the launch traced here: 189 us
  blocking collectives  103 us (54%)
  other arithmetic  28.5 us (15%)
  waiting for transfers between devices  26.2 us (14%)
  between operations  14.8 us (8%)
  matrix products  11.2 us (6%)
  local copies, waits for them, and re-layouts  3.92 us (2%)
    all_gather x2, blocking collectives, mix_works(): return all_gather(own_rows, net_axis).sum(axis=0)  61.2 us
    all_gather x1, waiting for transfers between devices, shards(): lax.all_gather(extended, 'frames', axis=0, tiled=True)  25.7 us
    psum x1, blocking collectives, shards(): count_rows = lax.psum(mult_rows, 'win')  21.3 us
    reduce_sum x1, other arithmetic, shards(): terms = gamma_rows * jnp.sum(ratios * mult_full[None, :], axis=1)  9.14 us
    reduce_sum x1, other arithmetic, shards(): new_rows = mult_rows * jnp.sum(ratios * scaled[None, :], axis=1)  8.99 us
    dot_general x1, matrix products, add_pair(): jnp.einsum('tr,ts->rs', later_cols, current, preferred_element_type=jnp.f...  8.77 us
    all_gather x1, blocking collectives, shards(): lax.all_gather(new_rows, 'frames', axis=0, tiled=True)  5.21 us
    all_gather x1, blocking collectives, shards(): lax.all_gather(raw_rows, 'frames', axis=0, tiled=True)  5.21 us
  transfers between devices with their start and end apart: 2, of which 2 were waited for; matrix products, arithmetic and copies ran while one was open for 2% of the time, Pallas kernels for 0%

profile of v1, /device:TPU:0, one launch (start us, length us, event | category | flops | bytes accessed | tf_op | source)
XLA Modules:
  0.0 189.3 jit_solution(8113734344410783831)
XLA Ops:
  7.2 0.0 all-gather.4.cloned.1.call-start
  7.2 1.3 convert_element_type.11
  8.5 1.3 collective-permute-start
  9.8 1.3 convert_bitcast_fusion
  11.1 0.6 collective-permute-done
  11.7 0.9 pad_maximum_fusion
  12.5 0.0 all-gather.4.cloned.1.call-update
  13.2 0.8 broadcast_multiply_fusion
  14.0 0.8 fusion.6
  14.8 25.7 %all-gather.4.cloned.1.call-done = bf16[288,4096]{1,0:T(8,128)(2,1)} async-done(((bf16[72,4096]{1,0:T(8,128)(2,1)}), bf16[288,4096]{1,0:T(8,128)(2,1)}) %all-gather.4.cloned.1.call-update) | async-done | bytes 2359312 | tf_op jit(solution)/shard_map/all_gather | solution.py:64
  40.5 2.9 %fusion.10 = (bf16[4,64,4096]{2,1,0:T(8,128)(2,1)S(1)}, bf16[4,64,4096]{2,1,0:T(8,128)(2,1)S(1)}) fusion(bf16[4,72,4096]{2,1,0:T(8,128)(2,1)} %bitcast.23, s32[]{:T(128)S(6)} %select_n.20), kind=kLoop, calls=%fused_computation.30 | loop fusion | bytes 8388612 | tf_op jit(solution)/shard_map/slice | solution.py:31
  43.4 0.0 copy-start
  43.4 0.4 bitcast_select_fusion
  43.8 0.9 copy-done
  44.8 2.4 %fusion.1 = f32[1024,4096]{1,0:T(8,128)S(1)} fusion(bf16[256,4096]{1,0:T(8,128)(2,1)S(1)} %bitcast_select_fusion, bf16[256,4096]{1,0:T(8,128)(2,1)S(1)} %bitcast.21, s32[]{:T(128)S(6)} %select_n.18), kind=kOutput, calls=%fused_computation.10 | convolution fusion | flops 2147483648 | bytes 19398660 | tf_op jit(solution)/shard_map/tr,ts->rs/dot_general | solution.py:42
  47.2 8.8 %fusion.11 = (f32[1024]{0:T(1024)S(1)}, f32[1024,4096]{1,0:T(8,128)}) fusion(f32[1024,4096]{1,0:T(8,128)S(1)} %fusion.1, bf16[256,4096]{1,0:T(8,128)(2,1)} %bitcast.22, bf16[256,4096]{1,0:T(8,128)(2,1)S(1)} %bitcast_select_fusion, s32[]{:T(128)S(6)} %select_n.18), kind=kOutput, calls=%fused_computation.31 | convolution fusion | flops 2155871232 | bytes 36179972 | tf_op jit(solution)/shard_map/tr,ts->rs/dot_general | solution.py:43
  56.0 5.2 %all_gather.28 = f32[4096]{0:T(1024)S(1)} all-gather(f32[1024]{0:T(1024)S(1)} %broadcast_multiply_fusion.1), channel_id=1, replica_groups=mesh['frames'=4,'win'=8] {'frames'}, dimensions={0}, use_global_device_ids=true | all-gather | bytes 20480 | tf_op jit(solution)/shard_map/all_gather | solution.py:70
  61.2 21.3 %psum.7 = f32[1024]{0:T(1024)S(1)} all-reduce(f32[1024]{0:T(1024)S(1)} %broadcast_multiply_fusion.1), channel_id=1, replica_groups=mesh['frames'=4,'win'=8] {'win'}, use_global_device_ids=true, to_apply=%region_1.2 | all-reduce | flops 1024 | bytes 8192 | tf_op jit(solution)/shard_map/psum | solution.py:72
  82.5 9.1 %multiply_reduce_fusion.2 = (f32[1024]{0:T(1024)S(1)}, f32[1024]{0:T(1024)S(1)}) fusion(f32[4096]{0:T(1024)S(1)} %all_gather.28, f32[4096]{0:T(1024)S(1)} %bitcast.26, f32[1024,4096]{1,0:T(8,128)} %get-tuple-element.11, f32[1024]{0:T(1024)S(1)} %dynamic-slice_multiply_fusion, f32[1024]{0:T(1024)S(1)} %broadcast_multiply_fusion.1), kind=kLoop, calls=%fused_computation.3 | loop fusion | flops 33552384 | bytes 16826368 | tf_op jit(solution)/shard_map/reduce_sum | solution.py:80
  91.7 5.2 %all_gather.32 = f32[4096]{0:T(1024)S(1)} all-gather(f32[1024]{0:T(1024)S(1)} %fusion.9), channel_id=1, replica_groups=mesh['frames'=4,'win'=8] {'frames'}, dimensions={0}, use_global_device_ids=true | all-gather | bytes 20480 | tf_op jit(solution)/shard_map/all_gather | solution.py:86
  96.9 30.6 %all-gather = f32[8192]{0:T(1024)S(1)} all-gather(f32[1024]{0:T(1024)S(1)} %mul.185), channel_id=2, replica_groups=mesh['frames'=4,'win'=8] {'win'}, dimensions={0}, use_global_device_ids=true | all-gather | bytes 36864 | tf_op jit(solution)/shard_map/all_gather | solution.py:14
  127.5 0.6 reduce_sum.99
  128.1 5.2 %all_gather.31 = f32[4096]{0:T(1024)S(1)} all-gather(f32[1024]{0:T(1024)S(1)} %div.38), channel_id=1, replica_groups=mesh['frames'=4,'win'=8] {'frames'}, dimensions={0}, use_global_device_ids=true | all-gather | bytes 20480 | tf_op jit(solution)/shard_map/all_gather | solution.py:85
  133.3 0.6 reduce_sum.94
  133.9 0.7 divide_multiply_fusion
  134.6 9.0 %multiply_reduce_fusion = (f32[1024]{0:T(1024)S(1)}, f32[1024]{0:T(1024)S(1)}) fusion(f32[4096]{0:T(1024)S(1)} %divide_multiply_fusion, f32[4096]{0:T(1024)S(1)} %all_gather.32, f32[1024,4096]{1,0:T(8,128)} %get-tuple-element.11, f32[1024]{0:T(1024)S(1)} %dynamic_slice.33, f32[1024]{0:T(1024)S(1)} %fusion.9), kind=kLoop, calls=%fused_computation | loop fusion | flops 33552384 | bytes 16826368 | tf_op jit(solution)/shard_map/reduce_sum | solution.py:79
  143.6 30.6 %all-gather.1 = f32[8192]{0:T(1024)S(1)} all-gather(f32[1024]{0:T(1024)S(1)} %mul.193), channel_id=3, replica_groups=mesh['frames'=4,'win'=8] {'win'}, dimensions={0}, use_global_device_ids=true | all-gather | bytes 36864 | tf_op jit(solution)/shard_map/all_gather | solution.py:14
  174.2 5.2 %all_gather.35 = f32[4096]{0:T(1024)S(1)} all-gather(f32[1024]{0:T(1024)S(1)} %div.42), channel_id=1, replica_groups=mesh['frames'=4,'win'=8] {'frames'}, dimensions={0}, use_global_device_ids=true | all-gather | bytes 20480 | tf_op jit(solution)/shard_map/all_gather | solution.py:89
  179.4 0.6 reduce_sum.97
  180.0 1.3 fusion.5
  181.3 1.2 divide_log_fusion
  (14 shorter events, 0.1 us)
Async XLA Ops:
  7.2 33.3 %all-gather.4.cloned.1.call-start = ((), (), s32[]{:S(2)}) async-start(), calls=%async_computation | async-start | bytes 2949120 | tf_op jit(solution)/shard_map/all_gather | solution.py:64
  8.5 3.1 %collective-permute-start = (bf16[8,4096]{1,0:T(8,128)(2,1)S(1)}, bf16[8,4096]{1,0:T(8,128)(2,1)S(1)}, u32[]{:S(2)}, u32[]{:S(2)}) collective-permute-start(bf16[8,4096]{1,0:T(8,128)(2,1)S(1)} %slice_bitcast_fusion), channel_id=1, source_target_pairs={{8,0},{16,8},{24,16},{9,1},{17,9},{25,17},{10,2},{18,10},{26,18},{... | collective-permute-start | bytes 196616 | tf_op jit(solution)/shard_map/ppermute | solution.py:23
  43.4 1.4 copy-start
Sparse Core Ops, SparseCore 0:
  12.7 27.7 all-gather.3
